TPU v7x, 32 devices: a whole 2x2x4 slice. The times are simulated.
32 devices in a mesh: seq: 8 (over z, x), head: 4 (over y, core), batch: 1.
Axes of the slice: x: 2, y: 2, z: 4, core: 2. Of those that a mesh axis runs over, the one named last changes fastest.
Arguments:
- queries: bfloat16 [2048, 4096], P(('batch', 'seq', 'head')), may hold values from -6 to 6
- keys: bfloat16 [2048, 512], P(('batch', 'seq', 'head')), may hold values from -6 to 6
- values: bfloat16 [2048, 512], P(('batch', 'seq', 'head')), may hold values from -6 to 6
- page_of_block: int32 [4], P('batch'), may hold values from 0 to 2, never falling along the last dimension, each value on 1 to 2 neighbouring positions
- links: int32 [4, 4], P('batch'), may hold values 0 or 1
Outputs:
- attended: bfloat16 [2048, 4096], P(('batch', 'seq', 'head'))
Inputs may be any that keep to these rules, and one draw needn't show every extreme that they name: `page_of_block`: page numbers never fall from one block to the next.
All inputs are finite; a program needn't handle non-finite values.
Results may differ from a plain program's by a relative error of at most 0.0065.
Values may be sent and summed in bfloat16 or wider, within the bound.
No kernel may reach another device: no remote copies, remote signals or barrier semaphores. Data moves between devices by JAX's collectives and lax.ppermute only.
A program may use at most 64 MiB of HBM per device.

v0:
```python
import jax
import jax.numpy as jnp
from jax import lax
from jax.sharding import PartitionSpec as P

HEAD_SIZE = 128
BLK = 512


def local(queries, keys, values, page_of_block, links):
    query_all, key_local, value_local = (
        lax.all_to_all(queries, "head", split_axis=1, concat_axis=0, tiled=True),
        lax.all_to_all(keys, "head", split_axis=1, concat_axis=0, tiled=True),
        lax.all_to_all(values, "head", split_axis=1, concat_axis=0, tiled=True),
    )
    row_count = query_all.shape[0]
    kv_here = key_local.shape[1] // HEAD_SIZE
    group_width = query_all.shape[1] // HEAD_SIZE // kv_here
    first_row = lax.axis_index("seq") * row_count
    block_count = page_of_block.shape[0]
    block_ids = jnp.arange(block_count, dtype=jnp.int32)
    page_table = page_of_block.astype(jnp.float32)
    link_table = links.astype(jnp.float32)
    query_pos = first_row + jnp.arange(row_count, dtype=jnp.int32)
    query_onehot = (query_pos[:, None] // BLK == block_ids[None, :]).astype(jnp.float32)
    query_page = jnp.dot(query_onehot, page_table, precision=lax.Precision.HIGHEST)
    query_links = jnp.dot(query_onehot, link_table, precision=lax.Precision.HIGHEST)
    query_heads = query_all.reshape(row_count, kv_here, group_width, HEAD_SIZE)
    score_scale = HEAD_SIZE ** (-0.5)

    def block_step(running, key_block, value_block, offset):
        block_rows = key_block.shape[0]
        key_pos = offset + jnp.arange(block_rows, dtype=jnp.int32)
        key_onehot = (key_pos[:, None] // BLK == block_ids[None, :]).astype(jnp.float32)
        key_page = jnp.dot(key_onehot, page_table, precision=lax.Precision.HIGHEST)
        linked = jnp.dot(query_links, key_onehot.T, precision=lax.Precision.HIGHEST) > 0.5
        same_page = query_page[:, None] == key_page[None, :]
        allowed = jnp.where(same_page, key_pos[None, :] <= query_pos[:, None], linked)

        def attend(previous):
            maxima, totals, weighted = previous
            scores = (
                jnp.einsum(
                    "rkgd,pkd->kgrp",
                    query_heads,
                    key_block.reshape(block_rows, kv_here, HEAD_SIZE),
                    preferred_element_type=jnp.float32,
                )
                * score_scale
            )
            scores = jnp.where(allowed[None, None], scores, -1e30)
            new_max = jnp.maximum(maxima, jnp.max(scores, axis=-1))
            weights = jnp.where(allowed[None, None], jnp.exp(scores - new_max[..., None]), 0.0)
            factor = jnp.exp(maxima - new_max)
            totals = totals * factor + jnp.sum(weights, axis=-1)
            rounded = weights.astype(jnp.bfloat16)
            weighted = weighted * factor[..., None] + jnp.einsum(
                "kgrp,pkd->kgrd",
                rounded,
                value_block.reshape(block_rows, kv_here, HEAD_SIZE),
                preferred_element_type=jnp.float32,
            )
            return (new_max, totals, weighted)

        return lax.cond(jnp.any(allowed), attend, lambda previous: previous, running)

    initial = (
        jnp.full((kv_here, group_width, row_count), -1e30, jnp.float32),
        jnp.zeros((kv_here, group_width, row_count), jnp.float32),
        jnp.zeros((kv_here, group_width, row_count, HEAD_SIZE), jnp.float32),
    )
    running = initial
    key_piece = lax.all_gather(key_local, "seq", axis=0, tiled=True)
    value_piece = lax.all_gather(value_local, "seq", axis=0, tiled=True)
    piece_rows = key_piece.shape[0]
    sub_count = piece_rows // BLK
    key_split = key_piece.reshape(sub_count, BLK, key_piece.shape[1])
    value_split = value_piece.reshape(sub_count, BLK, value_piece.shape[1])

    def scan_step(state_now, scan_item):
        key_block, value_block, block_index = scan_item
        return (block_step(state_now, key_block, value_block, block_index * BLK), None)

    running, unused = lax.scan(
        scan_step, running, (key_split, value_split, jnp.arange(sub_count, dtype=jnp.int32))
    )
    maxima, totals, weighted = running
    outcome = weighted / totals[..., None]
    outcome = (
        outcome.transpose(2, 0, 1, 3)
        .reshape(row_count, kv_here * group_width * HEAD_SIZE)
        .astype(jnp.bfloat16)
    )
    return lax.all_to_all(outcome, "head", split_axis=0, concat_axis=1, tiled=True)


def solution(mesh):
    in_specs = (
        P(("batch", "seq", "head"), None),
        P(("batch", "seq", "head"), None),
        P(("batch", "seq", "head"), None),
        P("batch"),
        P("batch", None),
    )
    out_specs = P(("batch", "seq", "head"), None)
    return jax.shard_map(local, mesh=mesh, in_specs=in_specs, out_specs=out_specs, check_vma=False)
```

profile of v0, /device:TPU:0, one launch (start us, length us, event | category | flops | bytes accessed | tf_op | source)
XLA Modules:
  0.0 122.0 jit_solution(15843513809518971838)
XLA Ops:
  0.0 0.0 copy-start
  0.0 0.8 copy-done
  0.8 0.6 copy_bitcast_fusion.2
  1.5 4.3 %all-to-all-start = ((bf16[64,4,128]{2,0,1:T(8,128)(2,1)}), bf16[64,4,128]{2,0,1:T(8,128)(2,1)S(1)}, u32[]{:S(2)}, u32[]{:S(2)}) async-start(bf16[64,4,128]{2,0,1:T(8,128)(2,1)} %copy_bitcast_fusion.2), calls=%async_computation | async-start | bytes 131072 | tf_op jit(solution)/shard_map/all_to_all | solution.py:13
  5.8 1.5 %copy_bitcast_fusion.1 = bf16[64,4,128]{2,0,1:T(8,128)(2,1)} fusion(bf16[64,512]{1,0:T(8,128)(2,1)} %param.11), kind=kLoop, calls=%fused_computation.53 | loop fusion | bytes 131072 | tf_op jit(solution)/shard_map/all_to_all | solution.py:14
  7.2 0.9 fusion.41
  8.1 1.7 %all-to-all-done = bf16[64,4,128]{2,0,1:T(8,128)(2,1)S(1)} async-done(((bf16[64,4,128]{2,0,1:T(8,128)(2,1)}), bf16[64,4,128]{2,0,1:T(8,128)(2,1)S(1)}, u32[]{:S(2)}, u32[]{:S(2)}) %all-to-all-start) | async-done | bytes 65568 | tf_op jit(solution)/shard_map/all_to_all | solution.py:13
  9.9 3.3 %all-to-all-start.2 = ((bf16[64,4,128]{2,0,1:T(8,128)(2,1)}), bf16[64,4,128]{2,0,1:T(8,128)(2,1)S(1)}, u32[]{:S(2)}, u32[]{:S(2)}) async-start(bf16[64,4,128]{2,0,1:T(8,128)(2,1)} %copy_bitcast_fusion.1), calls=%async_computation.2 | async-start | bytes 131072 | tf_op jit(solution)/shard_map/all_to_all | solution.py:14
  13.2 0.8 fusion.42
  14.0 0.7 convert_element_type.31
  14.7 1.9 %copy.43 = bf16[8,4,8,1024]{3,2,0,1:T(8,128)(2,1)} copy(bf16[8,4,8,1024]{3,2,1,0:T(8,128)(2,1)} %bitcast.120) | data formatting | bytes 1048576 | tf_op jit(solution)/shard_map/all_to_all | solution.py:12
  16.6 0.6 all-to-all-done.2
  17.2 3.5 %all-to-all-start.1 = ((bf16[64,4,1024]{2,0,1:T(8,128)(2,1)}), bf16[64,4,1024]{2,0,1:T(8,128)(2,1)S(1)}, u32[]{:S(2)}, u32[]{:S(2)}) async-start(bf16[64,4,1024]{2,0,1:T(8,128)(2,1)} %bitcast.104), calls=%async_computation.1 | async-start | bytes 1048576 | tf_op jit(solution)/shard_map/all_to_all | solution.py:12
  20.7 32.4 %all_gather.6 = bf16[2048,128]{1,0:T(8,128)(2,1)S(1)} all-gather(bf16[256,128]{1,0:T(8,128)(2,1)S(1)} %bitcast.122), channel_id=1, replica_groups=mesh['seq'=8,'head'=4,'batch'=1] {'seq'}, dimensions={0}, use_global_device_ids=true | all-gather | bytes 589824 | tf_op jit(solution)/shard_map/all_gather | solution.py:73
  53.1 31.2 %all_gather.7 = bf16[2048,128]{1,0:T(8,128)(2,1)S(1)} all-gather(bf16[256,128]{1,0:T(8,128)(2,1)S(1)} %bitcast.123), channel_id=1, replica_groups=mesh['seq'=8,'head'=4,'batch'=1] {'seq'}, dimensions={0}, use_global_device_ids=true | all-gather | bytes 589824 | tf_op jit(solution)/shard_map/all_gather | solution.py:74
  84.3 0.0 all-to-all-done.1
  84.3 0.1 copy.39
  84.4 0.1 copy.31
  84.4 0.1 broadcast_in_dim.54
  84.5 23.9 %while.19 = (s32[]{:T(128)}, f32[1,8,256]{2,1,0:T(8,128)S(1)}, f32[1,8,256]{2,1,0:T(8,128)S(1)}, f32[1,8,256,128]{3,2,1,0:T(8,128)S(1)}, f32[256]{0:T(256)S(1)},...) while((s32[]{:T(128)}, f32[1,8,256]{2,1,0:T(8,128)S(1)}, ...), condition=%wide.region_6.7_spmd.clone.clone, body=%wide.region_0.6_spmd.clone.clone.sunk | while | flops 558016768 | bytes 16143707 | solution.py:84
  84.6 0.6 dynamic_slice.42
  85.8 0.3 fusion.60
  86.1 1.1 fusion.61
  87.9 3.5 %conditional.4 = ((f32[1,8,256]{2,1,0:T(8,128)S(1)}, f32[1,8,256]{2,1,0:T(8,128)S(1)}, f32[1,8,256,128]{3,2,1,0:T(8,128)S(1)})) conditional(s32[]{:T(128)} %convert_element_type.56, (f32[1,8,256]{2,1,0:T(8,128)S(1)}, f32[1,8,256]{2,1,0:T(8,128)S(1)}, f32[1,8,256,128]{3,2,1,0:T(8,128)S(1)}) %tuple.66, (pred[256,512]{0,1:T(8,128)(4,1)S(1)}, ...), branch_computations={%region_2.2_spmd, %region_3.5_spmd} | conditional | flops 551032832 | bytes 15990824 | solution.py:65
  87.9 0.8 fusion.2
  88.7 1.6 %fusion.12 = f32[1,8,256,128]{3,2,1,0:T(8,128)S(1)} fusion(f32[512,256,8]{1,0,2:T(8,128)S(1)} %get-tuple-element.409, f32[8,256]{1,0:T(8,128)S(1)} %bitcast.113, pred[256,512]{0,1:T(8,128)(4,1)S(1)} %get-tuple-element.245, f32[1,8,256,128]{3,2,1,0:T(8,128)S(1)} %get-tuple-element.250, f32[8,256]{1,0:T(8,128)S(1)} %get-tuple-element.406, ...), kind=kOutput, calls=%fused_computation.10 | convolution fusion | flops 274202624 | bytes 6569988 | tf_op jit(solution)/shard_map/while/body/eval_jaxpr/cond/branch_1_fun/kgrp,pkd->kgrd/dot_general | solution.py:57
  90.4 1.0 fusion.4
  91.4 0.6 dynamic_slice.42
  92.7 0.3 fusion.60
  93.0 1.1 fusion.61
  94.8 3.5 %conditional.4 = ((f32[1,8,256]{2,1,0:T(8,128)S(1)}, f32[1,8,256]{2,1,0:T(8,128)S(1)}, f32[1,8,256,128]{3,2,1,0:T(8,128)S(1)})) conditional(s32[]{:T(128)} %convert_element_type.56, (f32[1,8,256]{2,1,0:T(8,128)S(1)}, f32[1,8,256]{2,1,0:T(8,128)S(1)}, f32[1,8,256,128]{3,2,1,0:T(8,128)S(1)}) %tuple.66, (pred[256,512]{0,1:T(8,128)(4,1)S(1)}, ...), branch_computations={%region_2.2_spmd, %region_3.5_spmd} | conditional | flops 551032832 | bytes 15990824 | solution.py:65
  94.8 0.8 fusion.2
  95.6 1.6 %fusion.12 = f32[1,8,256,128]{3,2,1,0:T(8,128)S(1)} fusion(f32[512,256,8]{1,0,2:T(8,128)S(1)} %get-tuple-element.409, f32[8,256]{1,0:T(8,128)S(1)} %bitcast.113, pred[256,512]{0,1:T(8,128)(4,1)S(1)} %get-tuple-element.245, f32[1,8,256,128]{3,2,1,0:T(8,128)S(1)} %get-tuple-element.250, f32[8,256]{1,0:T(8,128)S(1)} %get-tuple-element.406, ...), kind=kOutput, calls=%fused_computation.10 | convolution fusion | flops 274202624 | bytes 6569988 | tf_op jit(solution)/shard_map/while/body/eval_jaxpr/cond/branch_1_fun/kgrp,pkd->kgrd/dot_general | solution.py:57
  97.2 1.0 fusion.4
  98.3 0.6 dynamic_slice.42
  99.5 0.3 fusion.60
  99.8 1.1 fusion.61
  101.7 0.6 dynamic_slice.42
  102.9 0.3 fusion.60
  103.2 1.1 fusion.61
  105.0 3.5 %conditional.4 = ((f32[1,8,256]{2,1,0:T(8,128)S(1)}, f32[1,8,256]{2,1,0:T(8,128)S(1)}, f32[1,8,256,128]{3,2,1,0:T(8,128)S(1)})) conditional(s32[]{:T(128)} %convert_element_type.56, (f32[1,8,256]{2,1,0:T(8,128)S(1)}, f32[1,8,256]{2,1,0:T(8,128)S(1)}, f32[1,8,256,128]{3,2,1,0:T(8,128)S(1)}) %tuple.66, (pred[256,512]{0,1:T(8,128)(4,1)S(1)}, ...), branch_computations={%region_2.2_spmd, %region_3.5_spmd} | conditional | flops 551032832 | bytes 15990824 | solution.py:65
  105.0 0.8 fusion.2
  105.8 1.6 %fusion.12 = f32[1,8,256,128]{3,2,1,0:T(8,128)S(1)} fusion(f32[512,256,8]{1,0,2:T(8,128)S(1)} %get-tuple-element.409, f32[8,256]{1,0:T(8,128)S(1)} %bitcast.113, pred[256,512]{0,1:T(8,128)(4,1)S(1)} %get-tuple-element.245, f32[1,8,256,128]{3,2,1,0:T(8,128)S(1)} %get-tuple-element.250, f32[8,256]{1,0:T(8,128)S(1)} %get-tuple-element.406, ...), kind=kOutput, calls=%fused_computation.10 | convolution fusion | flops 274202624 | bytes 6569988 | tf_op jit(solution)/shard_map/while/body/eval_jaxpr/cond/branch_1_fun/kgrp,pkd->kgrd/dot_general | solution.py:57
  107.4 1.0 fusion.4
  108.5 0.3 fusion.40
  108.9 0.3 copy.32
  109.2 0.2 convert_element_type.35
  109.4 11.7 %all_to_all.70 = bf16[4,64,1024]{2,1,0:T(8,128)(2,1)S(1)} all-to-all(bf16[4,64,1024]{2,1,0:T(8,128)(2,1)S(1)} %convert_element_type.35), channel_id=1, replica_groups=mesh['seq'=8,'head'=4,'batch'=1] {'head'}, dimensions={0} | all-to-all | bytes 1048576 | tf_op jit(solution)/shard_map/all_to_all | solution.py:94
  121.2 0.8 copy.38
  (22 shorter events, 0.2 us)
Async XLA Ops:
  0.0 0.8 copy-start
  1.5 8.4 %all-to-all-start = ((bf16[64,4,128]{2,0,1:T(8,128)(2,1)}), bf16[64,4,128]{2,0,1:T(8,128)(2,1)S(1)}, u32[]{:S(2)}, u32[]{:S(2)}) async-start(bf16[64,4,128]{2,0,1:T(8,128)(2,1)} %copy_bitcast_fusion.2), calls=%async_computation | async-start | bytes 131072 | tf_op jit(solution)/shard_map/all_to_all | solution.py:13
  9.9 7.4 %all-to-all-start.2 = ((bf16[64,4,128]{2,0,1:T(8,128)(2,1)}), bf16[64,4,128]{2,0,1:T(8,128)(2,1)S(1)}, u32[]{:S(2)}, u32[]{:S(2)}) async-start(bf16[64,4,128]{2,0,1:T(8,128)(2,1)} %copy_bitcast_fusion.1), calls=%async_computation.2 | async-start | bytes 131072 | tf_op jit(solution)/shard_map/all_to_all | solution.py:14
  17.2 67.0 %all-to-all-start.1 = ((bf16[64,4,1024]{2,0,1:T(8,128)(2,1)}), bf16[64,4,1024]{2,0,1:T(8,128)(2,1)S(1)}, u32[]{:S(2)}, u32[]{:S(2)}) async-start(bf16[64,4,1024]{2,0,1:T(8,128)(2,1)} %bitcast.104), calls=%async_computation.1 | async-start | bytes 1048576 | tf_op jit(solution)/shard_map/all_to_all | solution.py:12
where the time goes:
time: 123 us; the launch traced here: 122 us
  blocking collectives  75.2 us (61%)
  matrix products  14.7 us (12%)
  starting transfers between devices  11 us (9%)
  local copies, waits for them, and re-layouts  8.84 us (7%)
  loops' own time  5.51 us (4%)
  other arithmetic  4.22 us (3%)
  waiting for transfers between devices  2.38 us (2%)
    all_gather x1, blocking collectives, local(): key_piece = lax.all_gather(key_local, 'seq', axis=0, tiled=True)  32.4 us
    all_gather x1, blocking collectives, local(): value_piece = lax.all_gather(value_local, 'seq', axis=0, tiled=True)  31.2 us
    all_to_all x1, blocking collectives, local(): lax.all_to_all(outcome, 'head', split_axis=0, concat_axis=1, tiled=True)  11.7 us
    another operation x1, loops' own time, local(): lax.scan(scan_step, running, (key_split, value_split, jnp.arange(sub_coun...  5.34 us
    dot_general x3, matrix products, attend(): jnp.einsum('kgrp,pkd->kgrd', rounded, value_block.reshape(block_rows, kv_...  4.83 us
    dot_general x4, matrix products, block_step(): jnp.dot(query_links, key_onehot.T, precision=lax.Precision.HIGHEST) > 0.5  4.53 us
    all_to_all x1, starting transfers between devices, local(): lax.all_to_all(keys, 'head', split_axis=1, concat_axis=0, tiled=True)  4.26 us
    all_to_all x1, starting transfers between devices, local(): lax.all_to_all(queries, 'head', split_axis=1, concat_axis=0, tiled=True)  3.47 us
  transfers between devices with their start and end apart: 3, of which 2 were waited for; matrix products, arithmetic and copies ran while one was open for 5% of the time, Pallas kernels for 0%

commit v1 on v0

--- a/solution.py
+++ b/solution.py
@@ -70,8 +70,13 @@
         jnp.zeros((kv_here, group_width, row_count, HEAD_SIZE), jnp.float32),
     )
     running = initial
-    key_piece = lax.all_gather(key_local, "seq", axis=0, tiled=True)
-    value_piece = lax.all_gather(value_local, "seq", axis=0, tiled=True)
+    key_piece, value_piece = jnp.split(
+        lax.all_gather(
+            jnp.concatenate([key_local, value_local], axis=1), "seq", axis=0, tiled=True
+        ),
+        [key_local.shape[1]],
+        axis=1,
+    )
     piece_rows = key_piece.shape[0]
     sub_count = piece_rows // BLK
     key_split = key_piece.reshape(sub_count, BLK, key_piece.shape[1])

time: 123 us -> 111 us (0.902)
  blocking collectives: 75.2 us -> 17.8 us
  waiting for transfers between devices: 2.38 us -> 36.6 us
  between operations: 0.1 us -> 13.5 us
  starting transfers between devices: 11 us -> 7.74 us
    all_gather x2 -> x0, blocking collectives: 63.5 us -> none  [the longest x1 32.4 us: local(): key_piece = lax.all_gather(key_local, 'seq', axis=0, tiled=True)]
    all_gather x0 -> x1, waiting for transfers between devices: none -> 27 us  [local(): lax.all_gather(jnp.concatenate([key_local, value_local], axis=1), 'seq',...]
    all_to_all x0 -> x1, blocking collectives: none -> 6.47 us  [local(): lax.all_to_all(values, 'head', split_axis=1, concat_axis=0, tiled=True)]
    all_to_all x1, waiting for transfers between devices: 0.01 us -> 6.3 us  [local(): lax.all_to_all(queries, 'head', split_axis=1, concat_axis=0, tiled=True)]
    all_to_all x1 -> x0, starting transfers between devices: 3.28 us -> none  [local(): lax.all_to_all(values, 'head', split_axis=1, concat_axis=0, tiled=True)]
    all_to_all x1, waiting for transfers between devices: 1.74 us -> 3.27 us  [local(): lax.all_to_all(keys, 'head', split_axis=1, concat_axis=0, tiled=True)]
    split x0 -> x1, local copies, waits for them, and re-layouts: none -> 1.27 us  [local(): jnp.split(lax.all_gather(jnp.concatenate([key_local, value_local], axis=1...]
  transfers between devices with their start and end apart: 3 -> 3, of which waited for: 2 -> 3; matrix products, arithmetic and copies ran while one was open for 5% -> 5% of each run, Pallas kernels for 0% -> 0%
where the time goes in v1:
time: 111 us; the launch traced here: 110 us
  waiting for transfers between devices  36.6 us (33%)
  blocking collectives  17.8 us (16%)
  matrix products  14.7 us (13%)
  between operations  13.5 us (12%)
  local copies, waits for them, and re-layouts  9.48 us (9%)
  starting transfers between devices  7.74 us (7%)
  loops' own time  5.51 us (5%)
  other arithmetic  4.83 us (4%)
    all_gather x1, waiting for transfers between devices, local(): lax.all_gather(jnp.concatenate([key_local, value_local], axis=1), 'seq',...  27 us
    all_to_all x1, blocking collectives, local(): lax.all_to_all(outcome, 'head', split_axis=0, concat_axis=1, tiled=True)  11.4 us
    all_to_all x1, blocking collectives, local(): lax.all_to_all(values, 'head', split_axis=1, concat_axis=0, tiled=True)  6.47 us
    all_to_all x1, waiting for transfers between devices, local(): lax.all_to_all(queries, 'head', split_axis=1, concat_axis=0, tiled=True)  6.3 us
    another operation x1, loops' own time, local(): lax.scan(scan_step, running, (key_split, value_split, jnp.arange(sub_coun...  5.34 us
    dot_general x3, matrix products, attend(): jnp.einsum('kgrp,pkd->kgrd', rounded, value_block.reshape(block_rows, kv_...  4.84 us
    dot_general x4, matrix products, block_step(): jnp.dot(query_links, key_onehot.T, precision=lax.Precision.HIGHEST) > 0.5  4.53 us
    all_to_all x1, starting transfers between devices, local(): lax.all_to_all(keys, 'head', split_axis=1, concat_axis=0, tiled=True)  4.26 us
  transfers between devices with their start and end apart: 3, of which 3 were waited for; matrix products, arithmetic and copies ran while one was open for 5% of the time, Pallas kernels for 0%

profile of v1, /device:TPU:0, one launch (start us, length us, event | category | flops | bytes accessed | tf_op | source)
XLA Modules:
  0.0 110.2 jit_solution(3970051429221018084)
XLA Ops:
  6.5 0.0 copy-start
  6.5 0.8 copy-done
  7.4 0.6 copy_bitcast_fusion.2
  8.0 4.3 %all-to-all-start = ((bf16[64,4,128]{2,0,1:T(8,128)(2,1)}), bf16[64,4,128]{2,0,1:T(8,128)(2,1)S(1)}, u32[]{:S(2)}, u32[]{:S(2)}) async-start(bf16[64,4,128]{2,0,1:T(8,128)(2,1)} %copy_bitcast_fusion.2), calls=%async_computation | async-start | bytes 131072 | tf_op jit(solution)/shard_map/all_to_all | solution.py:13
  12.3 0.0 all-gather.2.cloned.1.call-start
  12.3 0.9 copy_bitcast_fusion.1
  13.1 3.3 %all-to-all-done = bf16[64,4,128]{2,0,1:T(8,128)(2,1)S(1)} async-done(((bf16[64,4,128]{2,0,1:T(8,128)(2,1)}), bf16[64,4,128]{2,0,1:T(8,128)(2,1)S(1)}, u32[]{:S(2)}, u32[]{:S(2)}) %all-to-all-start) | async-done | bytes 65568 | tf_op jit(solution)/shard_map/all_to_all | solution.py:13
  16.4 6.5 %all_to_all.70 = bf16[64,4,128]{2,0,1:T(8,128)(2,1)S(1)} all-to-all(bf16[64,4,128]{2,0,1:T(8,128)(2,1)S(1)} %copy_bitcast_fusion.1), channel_id=1, replica_groups=mesh['seq'=8,'head'=4,'batch'=1] {'head'}, dimensions={1} | all-to-all | bytes 131072 | tf_op jit(solution)/shard_map/all_to_all | solution.py:14
  22.9 0.7 pad_maximum_fusion
  23.6 0.0 all-gather.2.cloned.1.call-update
  23.6 1.9 %copy.43 = bf16[8,4,8,1024]{3,2,0,1:T(8,128)(2,1)} copy(bf16[8,4,8,1024]{3,2,1,0:T(8,128)(2,1)} %bitcast.119) | data formatting | bytes 1048576 | tf_op jit(solution)/shard_map/all_to_all | solution.py:12
  25.5 3.5 %all-to-all-start.2 = ((bf16[64,4,1024]{2,0,1:T(8,128)(2,1)}), bf16[64,4,1024]{2,0,1:T(8,128)(2,1)S(1)}, u32[]{:S(2)}, u32[]{:S(2)}) async-start(bf16[64,4,1024]{2,0,1:T(8,128)(2,1)} %bitcast.104), calls=%async_computation.2 | async-start | bytes 1048576 | tf_op jit(solution)/shard_map/all_to_all | solution.py:12
  28.9 0.7 convert_element_type.31
  29.6 0.9 fusion.42
  30.5 0.9 fusion.41
  31.4 6.3 %all-to-all-done.2 = bf16[64,4,1024]{2,0,1:T(8,128)(2,1)S(1)} async-done(((bf16[64,4,1024]{2,0,1:T(8,128)(2,1)}), bf16[64,4,1024]{2,0,1:T(8,128)(2,1)S(1)}, u32[]{:S(2)}, u32[]{:S(2)}) %all-to-all-start.2) | async-done | bytes 524320 | tf_op jit(solution)/shard_map/all_to_all | solution.py:12
  37.7 0.1 copy.39
  37.8 0.1 copy.31
  37.9 27.0 %all-gather.2.cloned.1.call-done = bf16[2048,256]{1,0:T(8,128)(2,1)} async-done(((bf16[256,256]{1,0:T(8,128)(2,1)}), bf16[2048,256]{1,0:T(8,128)(2,1)}) %all-gather.2.cloned.1.call-update) | async-done | bytes 1048592 | tf_op jit(solution)/shard_map/all_gather | solution.py:74
  64.9 1.3 %fusion.49 = (bf16[2048,128]{1,0:T(8,128)(2,1)S(1)}, bf16[2048,128]{1,0:T(8,128)(2,1)S(1)}) fusion(bf16[2048,256]{1,0:T(8,128)(2,1)} %all-gather.2.cloned.1.call-done), kind=kLoop, calls=%fused_computation.66 | loop fusion | bytes 2097152 | tf_op jit(solution)/shard_map/split | solution.py:73
  66.2 0.1 broadcast_in_dim.54
  66.3 24.0 %while.19 = (s32[]{:T(128)}, f32[1,8,256]{2,1,0:T(8,128)S(1)}, f32[1,8,256]{2,1,0:T(8,128)S(1)}, f32[1,8,256,128]{3,2,1,0:T(8,128)S(1)}, f32[256]{0:T(256)S(1)},...) while((s32[]{:T(128)}, f32[1,8,256]{2,1,0:T(8,128)S(1)}, ...), condition=%wide.region_6.7_spmd.clone.clone, body=%wide.region_0.6_spmd.clone.clone.sunk | while | flops 558016768 | bytes 16143707 | solution.py:89
  66.3 0.6 dynamic_slice.42
  67.5 0.3 fusion.61
  67.9 1.1 %fusion.62 = (pred[]{:T(512)}, pred[256,512]{0,1:T(8,128)(4,1)S(1)}) fusion(f32[256,4]{0,1:T(4,128)S(1)} %get-tuple-element.544, s32[4]{0:T(128)S(1)} %get-tuple-element.542, s32[512]{0:T(512)S(1)} %get-tuple-element.496, s32[256]{0:T(256)S(1)} %iota_add_fusion.3, s32[512]{0:T(512)S(1)} %get-tuple-element.497, f32[512]{0:T(512)S(1)} %bitcast.124, ...), kind=kOutput, calls=%fused_computation.65.clone.1 | convolution fusion | flops 6948863 | bytes 143377 | tf_op jit(solution)/shard_map/while/body/eval_jaxpr/dot_general | solution.py:36
  69.6 3.5 %conditional.4 = ((f32[1,8,256]{2,1,0:T(8,128)S(1)}, f32[1,8,256]{2,1,0:T(8,128)S(1)}, f32[1,8,256,128]{3,2,1,0:T(8,128)S(1)})) conditional(s32[]{:T(128)} %convert_element_type.56, (f32[1,8,256]{2,1,0:T(8,128)S(1)}, f32[1,8,256]{2,1,0:T(8,128)S(1)}, f32[1,8,256,128]{3,2,1,0:T(8,128)S(1)}) %tuple.67, (pred[256,512]{0,1:T(8,128)(4,1)S(1)}, ...), branch_computations={%region_2.2_spmd, %region_3.5_spmd} | conditional | flops 551032832 | bytes 15990824 | solution.py:65
  69.7 0.8 fusion.2
  70.5 1.6 %fusion.12 = f32[1,8,256,128]{3,2,1,0:T(8,128)S(1)} fusion(f32[512,256,8]{1,0,2:T(8,128)S(1)} %get-tuple-element.409, f32[8,256]{1,0:T(8,128)S(1)} %bitcast.113, pred[256,512]{0,1:T(8,128)(4,1)S(1)} %get-tuple-element.245, f32[1,8,256,128]{3,2,1,0:T(8,128)S(1)} %get-tuple-element.250, f32[8,256]{1,0:T(8,128)S(1)} %get-tuple-element.406, ...), kind=kOutput, calls=%fused_computation.10 | convolution fusion | flops 274202624 | bytes 6569988 | tf_op jit(solution)/shard_map/while/body/eval_jaxpr/cond/branch_1_fun/kgrp,pkd->kgrd/dot_general | solution.py:57
  72.1 1.0 fusion.4
  73.1 0.6 dynamic_slice.42
  74.4 0.3 fusion.61
  74.7 1.1 %fusion.62 = (pred[]{:T(512)}, pred[256,512]{0,1:T(8,128)(4,1)S(1)}) fusion(f32[256,4]{0,1:T(4,128)S(1)} %get-tuple-element.544, s32[4]{0:T(128)S(1)} %get-tuple-element.542, s32[512]{0:T(512)S(1)} %get-tuple-element.496, s32[256]{0:T(256)S(1)} %iota_add_fusion.3, s32[512]{0:T(512)S(1)} %get-tuple-element.497, f32[512]{0:T(512)S(1)} %bitcast.124, ...), kind=kOutput, calls=%fused_computation.65.clone.1 | convolution fusion | flops 6948863 | bytes 143377 | tf_op jit(solution)/shard_map/while/body/eval_jaxpr/dot_general | solution.py:36
  76.5 3.5 %conditional.4 = ((f32[1,8,256]{2,1,0:T(8,128)S(1)}, f32[1,8,256]{2,1,0:T(8,128)S(1)}, f32[1,8,256,128]{3,2,1,0:T(8,128)S(1)})) conditional(s32[]{:T(128)} %convert_element_type.56, (f32[1,8,256]{2,1,0:T(8,128)S(1)}, f32[1,8,256]{2,1,0:T(8,128)S(1)}, f32[1,8,256,128]{3,2,1,0:T(8,128)S(1)}) %tuple.67, (pred[256,512]{0,1:T(8,128)(4,1)S(1)}, ...), branch_computations={%region_2.2_spmd, %region_3.5_spmd} | conditional | flops 551032832 | bytes 15990824 | solution.py:65
  76.5 0.8 fusion.2
  77.3 1.6 %fusion.12 = f32[1,8,256,128]{3,2,1,0:T(8,128)S(1)} fusion(f32[512,256,8]{1,0,2:T(8,128)S(1)} %get-tuple-element.409, f32[8,256]{1,0:T(8,128)S(1)} %bitcast.113, pred[256,512]{0,1:T(8,128)(4,1)S(1)} %get-tuple-element.245, f32[1,8,256,128]{3,2,1,0:T(8,128)S(1)} %get-tuple-element.250, f32[8,256]{1,0:T(8,128)S(1)} %get-tuple-element.406, ...), kind=kOutput, calls=%fused_computation.10 | convolution fusion | flops 274202624 | bytes 6569988 | tf_op jit(solution)/shard_map/while/body/eval_jaxpr/cond/branch_1_fun/kgrp,pkd->kgrd/dot_general | solution.py:57
  78.9 1.0 fusion.4
  80.0 0.6 dynamic_slice.42
  81.3 0.3 fusion.61
  81.6 1.1 %fusion.62 = (pred[]{:T(512)}, pred[256,512]{0,1:T(8,128)(4,1)S(1)}) fusion(f32[256,4]{0,1:T(4,128)S(1)} %get-tuple-element.544, s32[4]{0:T(128)S(1)} %get-tuple-element.542, s32[512]{0:T(512)S(1)} %get-tuple-element.496, s32[256]{0:T(256)S(1)} %iota_add_fusion.3, s32[512]{0:T(512)S(1)} %get-tuple-element.497, f32[512]{0:T(512)S(1)} %bitcast.124, ...), kind=kOutput, calls=%fused_computation.65.clone.1 | convolution fusion | flops 6948863 | bytes 143377 | tf_op jit(solution)/shard_map/while/body/eval_jaxpr/dot_general | solution.py:36
  83.4 0.6 dynamic_slice.42
  84.6 0.3 fusion.61
  85.0 1.1 %fusion.62 = (pred[]{:T(512)}, pred[256,512]{0,1:T(8,128)(4,1)S(1)}) fusion(f32[256,4]{0,1:T(4,128)S(1)} %get-tuple-element.544, s32[4]{0:T(128)S(1)} %get-tuple-element.542, s32[512]{0:T(512)S(1)} %get-tuple-element.496, s32[256]{0:T(256)S(1)} %iota_add_fusion.3, s32[512]{0:T(512)S(1)} %get-tuple-element.497, f32[512]{0:T(512)S(1)} %bitcast.124, ...), kind=kOutput, calls=%fused_computation.65.clone.1 | convolution fusion | flops 6948863 | bytes 143377 | tf_op jit(solution)/shard_map/while/body/eval_jaxpr/dot_general | solution.py:36
  86.7 3.5 %conditional.4 = ((f32[1,8,256]{2,1,0:T(8,128)S(1)}, f32[1,8,256]{2,1,0:T(8,128)S(1)}, f32[1,8,256,128]{3,2,1,0:T(8,128)S(1)})) conditional(s32[]{:T(128)} %convert_element_type.56, (f32[1,8,256]{2,1,0:T(8,128)S(1)}, f32[1,8,256]{2,1,0:T(8,128)S(1)}, f32[1,8,256,128]{3,2,1,0:T(8,128)S(1)}) %tuple.67, (pred[256,512]{0,1:T(8,128)(4,1)S(1)}, ...), branch_computations={%region_2.2_spmd, %region_3.5_spmd} | conditional | flops 551032832 | bytes 15990824 | solution.py:65
  86.8 0.8 fusion.2
  87.6 1.6 %fusion.12 = f32[1,8,256,128]{3,2,1,0:T(8,128)S(1)} fusion(f32[512,256,8]{1,0,2:T(8,128)S(1)} %get-tuple-element.409, f32[8,256]{1,0:T(8,128)S(1)} %bitcast.113, pred[256,512]{0,1:T(8,128)(4,1)S(1)} %get-tuple-element.245, f32[1,8,256,128]{3,2,1,0:T(8,128)S(1)} %get-tuple-element.250, f32[8,256]{1,0:T(8,128)S(1)} %get-tuple-element.406, ...), kind=kOutput, calls=%fused_computation.10 | convolution fusion | flops 274202624 | bytes 6569988 | tf_op jit(solution)/shard_map/while/body/eval_jaxpr/cond/branch_1_fun/kgrp,pkd->kgrd/dot_general | solution.py:57
  89.2 1.0 fusion.4
  90.2 0.3 fusion.40
  90.6 0.3 copy.32
  90.9 0.2 convert_element_type.35
  91.2 11.4 %all_to_all.71 = bf16[4,64,1024]{2,1,0:T(8,128)(2,1)S(1)} all-to-all(bf16[4,64,1024]{2,1,0:T(8,128)(2,1)S(1)} %convert_element_type.35), channel_id=1, replica_groups=mesh['seq'=8,'head'=4,'batch'=1] {'head'}, dimensions={0} | all-to-all | bytes 1048576 | tf_op jit(solution)/shard_map/all_to_all | solution.py:99
  102.5 0.8 copy.38
  (22 shorter events, 0.2 us)
Async XLA Ops:
  6.5 0.8 copy-start
  8.0 8.4 %all-to-all-start = ((bf16[64,4,128]{2,0,1:T(8,128)(2,1)}), bf16[64,4,128]{2,0,1:T(8,128)(2,1)S(1)}, u32[]{:S(2)}, u32[]{:S(2)}) async-start(bf16[64,4,128]{2,0,1:T(8,128)(2,1)} %copy_bitcast_fusion.2), calls=%async_computation | async-start | bytes 131072 | tf_op jit(solution)/shard_map/all_to_all | solution.py:13
  12.3 52.6 %all-gather.2.cloned.1.call-start = ((), (), s32[]{:S(2)}) async-start(), calls=%async_computation.4 | async-start | bytes 1179648 | tf_op jit(solution)/shard_map/all_gather | solution.py:74
  25.5 12.3 %all-to-all-start.2 = ((bf16[64,4,1024]{2,0,1:T(8,128)(2,1)}), bf16[64,4,1024]{2,0,1:T(8,128)(2,1)S(1)}, u32[]{:S(2)}, u32[]{:S(2)}) async-start(bf16[64,4,1024]{2,0,1:T(8,128)(2,1)} %bitcast.104), calls=%async_computation.2 | async-start | bytes 1048576 | tf_op jit(solution)/shard_map/all_to_all | solution.py:12
Sparse Core Ops, SparseCore 0:
  23.7 41.1 all-gather.1
